TPU v7x, 128 devices: a whole 4x4x4 slice. The times are simulated.
128 devices in a mesh: role: 2 (over core), dev: 64 (over z, y, x).
Axes of the slice: x: 4, y: 4, z: 4, core: 2. Of those that a mesh axis runs over, the one named last changes fastest.
Arguments:
- moe_rows: bfloat16 [4096, 3584], P(('role', 'dev')), may hold values from -6 to 6
- expert_ids: int32 [4096, 8], P(('role', 'dev')), may hold values from 0 to 63, all different within a row; in each aligned block of 32 rows (0 to 31, 32 to 63, ...) at most 8 rows name the same one
- gate_weights: float32 [4096, 8], P(('role', 'dev')), may hold values from 0.05 to 0.6
- w_gate: bfloat16 [64, 3584, 1024], P('dev', None, 'role'), may hold values from -0.09375 to 0.09375
- w_up: bfloat16 [64, 3584, 1024], P('dev', None, 'role'), may hold values from -0.09375 to 0.09375
- w_down: bfloat16 [64, 3584, 1024], P('dev', None, 'role'), may hold values from -0.1875 to 0.1875
- q_latent: bfloat16 [512, 64, 512], P(('role', 'dev')), may hold values from -40 to 40
- q_rope: bfloat16 [512, 4096], P(('role', 'dev')), may hold values from -4 to 4
- latent_cache: bfloat16 [512, 2048, 512], P(('role', 'dev')), may hold values from -4 to 4
- rope_cache: bfloat16 [512, 64, 2048], P(('role', 'dev')), may hold values from -4 to 4
- lengths: int32 [512], P(('role', 'dev')), may hold values from 2 to 2048, as said below
Outputs:
- moe_out: bfloat16 [4096, 3584], P(('role', 'dev'))
- attended: bfloat16 [512, 64, 512], P(('role', 'dev'))
Inputs may be any that keep to these rules, and one draw needn't show every extreme that they name: `expert_ids`: each row names 8 different experts; among the rows of one device no expert is named more than 8 times. `lengths`: the first row holds all 2048 cached tokens.
All inputs are finite; a program needn't handle non-finite values.
Results may differ from a plain program's by a relative error of at most 0.0057.
Values may be sent and summed in bfloat16 or wider, within the bound.
A program may use at most 128 MiB of HBM per device.

v0:
```python
import jax
import jax.numpy as jnp
from jax import lax
from jax.sharding import PartitionSpec as P

score_scale = 192.0 ** (-0.5)


def expert_block(chosen, gate_matrix, up_matrix, down_matrix):
    gate_part = jnp.dot(chosen, gate_matrix, preferred_element_type=jnp.float32)
    up_part = jnp.dot(chosen, up_matrix, preferred_element_type=jnp.float32)
    hidden_units = (jax.nn.silu(gate_part) * up_part).astype(jnp.bfloat16)
    return lax.dot_general(
        hidden_units, down_matrix, (((1,), (1,)), ((), ())), preferred_element_type=jnp.float32
    )


def attend_row(query_lat, query_rope, cache_lat, cache_rope, length):
    head_count = query_lat.shape[0]
    rope_width = cache_rope.shape[0]
    scores = lax.dot_general(
        query_lat, cache_lat, (((1,), (1,)), ((), ())), preferred_element_type=jnp.float32
    )
    scores = scores + jnp.dot(
        query_rope.reshape(head_count, rope_width), cache_rope, preferred_element_type=jnp.float32
    )
    scores = scores * score_scale
    positions = jnp.arange(cache_lat.shape[0], dtype=jnp.int32)
    valid = (positions < length)[None, :]
    scores = jnp.where(valid, scores, jnp.float32(-1e30))
    highest = jnp.max(scores, axis=1, keepdims=True)
    weights = jnp.where(valid, jnp.exp(scores - highest), jnp.float32(0.0))
    probs = (weights / jnp.sum(weights, axis=1, keepdims=True)).astype(jnp.bfloat16)
    return jnp.dot(probs, cache_lat, preferred_element_type=jnp.float32).astype(jnp.bfloat16)


def per_device(
    moe_rows,
    expert_ids,
    gate_weights,
    w_gate,
    w_up,
    w_down,
    q_latent,
    q_rope,
    latent_cache,
    rope_cache,
    lengths,
):
    tok_count = moe_rows.shape[0]
    width = moe_rows.shape[1]
    topk_count = expert_ids.shape[1]
    experts = lax.axis_size("dev")
    capacity = min(tok_count, 2 * tok_count * topk_count // experts)
    flat_ids = expert_ids.reshape(-1)
    pair_count = flat_ids.shape[0]
    one_hot = (flat_ids[:, None] == jnp.arange(experts, dtype=jnp.int32)[None, :]).astype(jnp.int32)
    earlier = jnp.cumsum(one_hot, axis=0) - one_hot
    slot_index = jnp.sum(earlier * one_hot, axis=1)
    destination = flat_ids * capacity + slot_index
    source_row = jnp.full((experts * capacity,), tok_count, jnp.int32)
    source_row = source_row.at[destination].set(
        jnp.arange(pair_count, dtype=jnp.int32) // topk_count
    )
    padded_rows = jnp.concatenate([moe_rows, jnp.zeros((1, width), jnp.bfloat16)], axis=0)
    outgoing = padded_rows[source_row].reshape(experts, capacity, width)
    arrived = lax.all_to_all(outgoing, "dev", split_axis=0, concat_axis=0, tiled=True)
    own_rows = arrived.reshape(experts * capacity, width)
    both_rows = lax.all_gather(own_rows, "role", axis=0, tiled=True)
    expert_sum = lax.psum_scatter(
        expert_block(both_rows, w_gate[0], w_up[0], w_down[0]),
        "role",
        scatter_dimension=0,
        tiled=True,
    )
    finished = expert_sum.astype(jnp.bfloat16).reshape(experts, capacity, width)
    returned = lax.all_to_all(finished, "dev", split_axis=0, concat_axis=0, tiled=True)
    flat_back = returned.reshape(experts * capacity, width)
    picked = flat_back[destination].reshape(tok_count, topk_count, width).astype(jnp.float32)
    moe_out = jnp.sum(picked * gate_weights[:, :, None], axis=1).astype(jnp.bfloat16)
    attended = jax.vmap(attend_row)(q_latent, q_rope, latent_cache, rope_cache, lengths)
    return (moe_out, attended)


def solution(mesh):
    placed = (
        P(("role", "dev"), None),
        P(("role", "dev"), None),
        P(("role", "dev"), None),
        P("dev", None, "role"),
        P("dev", None, "role"),
        P("dev", None, "role"),
        P(("role", "dev"), None, None),
        P(("role", "dev"), None),
        P(("role", "dev"), None, None),
        P(("role", "dev"), None, None),
        P(("role", "dev")),
    )
    return jax.shard_map(
        per_device,
        mesh=mesh,
        in_specs=placed,
        out_specs=(P(("role", "dev"), None), P(("role", "dev"), None, None)),
        check_vma=False,
    )
```

profile of v0, /device:TPU:1, one launch (start us, length us, event | category | flops | bytes accessed | tf_op | source)
XLA Modules:
  0.0 223.4 jit_solution(7646429509567561305)
XLA Ops:
  7.2 0.8 copy.15
  8.1 0.1 eq.29
  8.2 0.7 broadcast_multiply_fusion
  9.0 0.6 reduce-window.6
  9.6 0.2 slice_reduce_fusion
  9.9 0.1 mul.42
  10.0 0.1 fusion.21
  10.1 1.4 scatter_custom_fusion
  11.5 1.0 concatenate.3
  12.5 4.2 %gather_fusion = bf16[512,3584]{1,0:T(8,128)(2,1)} fusion(bf16[33,3584]{1,0:T(8,128)(2,1)S(1)} %concatenate.3, s32[1024]{0:T(1024)S(1)} %pad_clamp_fusion.1), kind=kCustom, calls=%fused_computation | custom fusion | bytes 7342080 | tf_op jit(solution)/shard_map/gather | solution.py:66
  16.7 57.5 %all_to_all.10 = bf16[64,8,3584]{2,1,0:T(8,128)(2,1)} all-to-all(bf16[64,8,3584]{2,1,0:T(8,128)(2,1)} %bitcast.49), channel_id=1, replica_groups=mesh['role'=2,'dev'=64] {'dev'}, dimensions={0} | all-to-all | bytes 7340032 | tf_op jit(solution)/shard_map/all_to_all | solution.py:67
  74.3 19.5 %all-gather.2.cloned.1.call-done = bf16[1024,3584]{1,0:T(8,128)(2,1)} async-done(((bf16[512,3584]{1,0:T(8,128)(2,1)}), bf16[1024,3584]{1,0:T(8,128)(2,1)}) %all-gather.2.cloned.1.call-update) | async-done | bytes 7340048 | tf_op jit(solution)/shard_map/all_gather | solution.py:69
  93.8 7.3 %fusion.4 = f32[1024,512]{1,0:T(8,128)S(1)} fusion(bf16[1024,3584]{1,0:T(8,128)(2,1)} %all-gather.2.cloned.1.call-done, bf16[1,3584,512]{2,1,0:T(8,128)(2,1)} %param.15), kind=kOutput, calls=%fused_computation.8 | convolution fusion | flops 3758096384 | bytes 13107200 | tf_op jit(solution)/shard_map/dot_general | solution.py:11
  101.1 15.5 %fusion.2 = f32[1024,3584]{1,0:T(8,128)} fusion(bf16[1,3584,512]{2,1,0:T(8,128)(2,1)} %param.16, f32[1024,512]{1,0:T(8,128)S(1)} %fusion.4, bf16[1024,3584]{1,0:T(8,128)(2,1)} %all-gather.2.cloned.1.call-done, bf16[1,3584,512]{2,1,0:T(8,128)(2,1)} %param.14), kind=kOutput, calls=%fused_computation.6 | convolution fusion | flops 7519338496 | bytes 31457280 | tf_op jit(solution)/shard_map/dot_general | solution.py:13
  116.6 28.2 %reduce-scatter.2.cloned.1.call-done = f32[512,3584]{1,0:T(8,128)} async-done(((f32[1024,3584]{1,0:T(8,128)}), f32[512,3584]{1,0:T(8,128)}) %reduce-scatter.2.cloned.1.call-update) | async-done | bytes 7340048 | tf_op jit(solution)/shard_map/reduce_scatter | solution.py:70
  144.8 5.3 %convert_bitcast_fusion = bf16[64,8,3584]{2,1,0:T(8,128)(2,1)} fusion(f32[512,3584]{1,0:T(8,128)} %reduce-scatter.2.cloned.1.call-done), kind=kLoop, calls=%fused_computation.12 | loop fusion | flops 1835008 | bytes 11010048 | tf_op jit(solution)/shard_map/reshape | solution.py:76
  150.1 10.7 %all-to-all-start.1 = ((bf16[64,8,3584]{2,1,0:T(8,128)(2,1)}), bf16[64,8,3584]{2,1,0:T(8,128)(2,1)}, u32[]{:S(2)}, u32[]{:S(2)}) async-start(bf16[64,8,3584]{2,1,0:T(8,128)(2,1)} %convert_bitcast_fusion), calls=%async_computation.2 | async-start | bytes 7340032 | tf_op jit(solution)/shard_map/all_to_all | solution.py:77
  160.8 0.1 reshape.93
  161.1 6.0 %fusion.27 = f32[4,64,2048]{2,1,0:T(8,128)S(1)} fusion(bf16[4,64,512]{2,1,0:T(8,128)(2,1)S(1)} %copy-done.1, bf16[4,2048,512]{2,1,0:T(8,128)(2,1)} %param.19), kind=kOutput, calls=%fused_computation.47 | convolution fusion | flops 536870912 | bytes 10747904 | tf_op jit(solution)/shard_map/vmap()/dot_general | solution.py:21
  167.1 2.4 %fusion.26 = (f32[4,64]{1,0:T(4,128)S(1)}, f32[4,64,2048]{2,1,0:T(8,128)}) fusion(pred[4,2048]{1,0:T(4,128)(4,1)S(1)} %iota_compare_fusion.2, f32[4,64,2048]{2,1,0:T(8,128)S(1)} %fusion.27, bf16[4,64,64]{2,1,0:T(8,128)(2,1)S(1)} %reshape.93, bf16[4,64,2048]{2,1,0:T(8,128)(2,1)S(1)} %copy-done), kind=kOutput, calls=%fused_computation.46 | convolution fusion | flops 70256640 | bytes 5284864 | tf_op jit(solution)/shard_map/vmap()/sub | solution.py:32
  169.4 6.3 %convolution_convert_fusion = bf16[4,64,512]{2,1,0:T(8,128)(2,1)} fusion(bf16[4,2048,512]{2,1,0:T(8,128)(2,1)} %param.19, f32[4,64,2048]{2,1,0:T(8,128)} %get-tuple-element.3, f32[4,64]{1,0:T(4,128)S(1)} %get-tuple-element.2), kind=kOutput, calls=%fused_computation.21 | convolution fusion | flops 538050560 | bytes 10748928 | tf_op jit(solution)/shard_map/vmap()/dot_general | solution.py:34
  175.8 32.6 %all-to-all-done.1 = bf16[64,8,3584]{2,1,0:T(8,128)(2,1)} async-done(((bf16[64,8,3584]{2,1,0:T(8,128)(2,1)}), bf16[64,8,3584]{2,1,0:T(8,128)(2,1)}, u32[]{:S(2)}, u32[]{:S(2)}) %all-to-all-start.1) | async-done | bytes 3670048 | tf_op jit(solution)/shard_map/all_to_all | solution.py:77
  208.4 6.0 %gather_fusion.1 = bf16[256,3584]{1,0:T(8,128)(2,1)S(1)} fusion(bf16[512,3584]{1,0:T(8,128)(2,1)} %bitcast.9, s32[1024]{0:T(1024)S(1)} %pad_clamp_fusion), kind=kCustom, calls=%fused_computation.1 | custom fusion | bytes 3671040 | tf_op jit(solution)/shard_map/gather | solution.py:79
  214.5 2.1 fusion.1
  (26 shorter events, 0.5 us)
Async XLA Ops:
  7.2 159.9 %copy-start = (bf16[4,64,2048]{2,1,0:T(8,128)(2,1)S(1)}, bf16[4,64,2048]{2,1,0:T(8,128)(2,1)}, u32[]{:S(2)}) copy-start(bf16[4,64,2048]{2,1,0:T(8,128)(2,1)} %param.20) | copy-start | bytes 3145732
  7.2 86.6 %all-gather.2.cloned.1.call-start = ((), (), s32[]{:S(2)}) async-start(), calls=%async_computation.3 | async-start | bytes 11010048 | tf_op jit(solution)/shard_map/all_gather | solution.py:69
  74.2 70.5 %reduce-scatter.2.cloned.1.call-start = ((), (), s32[]{:S(2)}) async-start(), calls=%async_computation.4 | async-start | bytes 22020096 | tf_op jit(solution)/shard_map/reduce_scatter | solution.py:70
  150.1 10.7 %copy-start.3 = (f32[32,8]{0,1:T(8,128)S(1)}, f32[32,8]{0,1:T(8,128)}, u32[]{:S(2)}) copy-start(f32[32,8]{0,1:T(8,128)} %param.13) | copy-start | bytes 3076
  150.1 10.8 %copy-start.2 = (bf16[4,4096]{1,0:T(4,128)(2,1)S(1)}, bf16[4,4096]{1,0:T(4,128)(2,1)}, u32[]{:S(2)}) copy-start(bf16[4,4096]{1,0:T(4,128)(2,1)} %param.18) | copy-start | bytes 98308
  150.1 10.9 %copy-start.4 = (s32[4]{0:T(128)S(1)}, s32[4]{0:T(128)}, u32[]{:S(2)}) copy-start(s32[4]{0:T(128)} %param.21) | copy-start | bytes 52
  150.1 11.0 %copy-start.1 = (bf16[4,64,512]{2,1,0:T(8,128)(2,1)S(1)}, bf16[4,64,512]{2,1,0:T(8,128)(2,1)}, u32[]{:S(2)}) copy-start(bf16[4,64,512]{2,1,0:T(8,128)(2,1)} %param.17) | copy-start | bytes 786436
  150.1 58.3 %all-to-all-start.1 = ((bf16[64,8,3584]{2,1,0:T(8,128)(2,1)}), bf16[64,8,3584]{2,1,0:T(8,128)(2,1)}, u32[]{:S(2)}, u32[]{:S(2)}) async-start(bf16[64,8,3584]{2,1,0:T(8,128)(2,1)} %convert_bitcast_fusion), calls=%async_computation.2 | async-start | bytes 7340032 | tf_op jit(solution)/shard_map/all_to_all | solution.py:77
Sparse Core Ops, SparseCore 0:
  74.4 19.3 all-gather.1
  116.7 28.0 reduce-scatter.1
where the time goes:
time: 224 us; the launch traced here: 223 us
  waiting for transfers between devices  80.4 us (36%)
  blocking collectives  57.5 us (26%)
  matrix products  37.5 us (17%)
  local copies, waits for them, and re-layouts  14.2 us (6%)
  between operations  14.2 us (6%)
  starting transfers between devices  10.8 us (5%)
  other arithmetic  8.97 us (4%)
    all_to_all x1, blocking collectives, per_device(): lax.all_to_all(outgoing, 'dev', split_axis=0, concat_axis=0, tiled=True)  57.5 us
    all_to_all x1, waiting for transfers between devices, per_device(): lax.all_to_all(finished, 'dev', split_axis=0, concat_axis=0, tiled=True)  32.6 us
    reduce_scatter x1, waiting for transfers between devices, per_device(): lax.psum_scatter(expert_block(both_rows, w_gate[0], w_up[0], w_down[0]),...  28.2 us
    all_gather x1, waiting for transfers between devices, per_device(): both_rows = lax.all_gather(own_rows, 'role', axis=0, tiled=True)  19.5 us
    dot_general x1, matrix products, expert_block(): lax.dot_general(hidden_units, down_matrix, (((1,), (1,)), ((), ())), pref...  15.5 us
    all_to_all x1, starting transfers between devices, per_device(): lax.all_to_all(finished, 'dev', split_axis=0, concat_axis=0, tiled=True)  10.7 us
    dot_general x1, matrix products, expert_block(): up_part = jnp.dot(chosen, up_matrix, preferred_element_type=jnp.float32)  7.29 us
    dot_general x1, matrix products, attend_row(): jnp.dot(probs, cache_lat, preferred_element_type=jnp.float32)  6.34 us
  transfers between devices with their start and end apart: 3, of which 3 were waited for; matrix products, arithmetic and copies ran while one was open for 7% of the time, Pallas kernels for 0%

commit v1 on v0

--- a/solution.py
+++ b/solution.py
@@ -66,7 +66,9 @@
     outgoing = padded_rows[source_row].reshape(experts, capacity, width)
     arrived = lax.all_to_all(outgoing, "dev", split_axis=0, concat_axis=0, tiled=True)
     own_rows = arrived.reshape(experts * capacity, width)
-    both_rows = lax.all_gather(own_rows, "role", axis=0, tiled=True)
+    both_rows = jnp.concatenate(
+        lax.all_to_all(jnp.stack([own_rows] * lax.axis_size("role")), "role", 0, 0), axis=0
+    )
     expert_sum = lax.psum_scatter(
         expert_block(both_rows, w_gate[0], w_up[0], w_down[0]),
         "role",

time: 224 us -> 211 us (0.942)
  waiting for transfers between devices: 80.4 us -> 55.9 us
  blocking collectives: 57.5 us -> 69.3 us
  matrix products: 37.5 us -> 34.1 us
  local copies, waits for them, and re-layouts: 14.2 us -> 17.1 us
    all_gather x1 -> x0, waiting for transfers between devices: 19.5 us -> none  [per_device(): both_rows = lax.all_gather(own_rows, 'role', axis=0, tiled=True)]
    all_to_all x0 -> x1, blocking collectives: none -> 11.9 us  [per_device(): lax.all_to_all(jnp.stack([own_rows] * lax.axis_size('role')), 'role', 0, 0)]
    reduce_scatter x1, waiting for transfers between devices: 28.2 us -> 23.2 us  [per_device(): lax.psum_scatter(expert_block(both_rows, w_gate[0], w_up[0], w_down[0]),...]
    dot_general x1, matrix products: 7.29 us -> 3.93 us  [expert_block(): up_part = jnp.dot(chosen, up_matrix, preferred_element_type=jnp.float32)]
    unnamed x12 -> x16, local copies, waits for them, and re-layouts: 0.94 us -> 3.89 us
  transfers between devices with their start and end apart: 3 -> 2, of which waited for: 3 -> 2; matrix products, arithmetic and copies ran while one was open for 7% -> 7% of each run, Pallas kernels for 0% -> 0%
where the time goes in v1:
time: 211 us
  blocking collectives  69.3 us (33%)
  waiting for transfers between devices  55.9 us (26%)
  matrix products  34.1 us (16%)
  local copies, waits for them, and re-layouts  17.1 us (8%)
  between operations  14.2 us (7%)
  starting transfers between devices  10.7 us (5%)
  other arithmetic  9.6 us (5%)
    all_to_all x1, blocking collectives, per_device(): lax.all_to_all(outgoing, 'dev', split_axis=0, concat_axis=0, tiled=True)  57.4 us
    all_to_all x1, waiting for transfers between devices, per_device(): lax.all_to_all(finished, 'dev', split_axis=0, concat_axis=0, tiled=True)  32.6 us
    reduce_scatter x1, waiting for transfers between devices, per_device(): lax.psum_scatter(expert_block(both_rows, w_gate[0], w_up[0], w_down[0]),...  23.2 us
    dot_general x1, matrix products, expert_block(): lax.dot_general(hidden_units, down_matrix, (((1,), (1,)), ((), ())), pref...  15.5 us
    all_to_all x1, blocking collectives, per_device(): lax.all_to_all(jnp.stack([own_rows] * lax.axis_size('role')), 'role', 0, 0)  11.9 us
    all_to_all x1, starting transfers between devices, per_device(): lax.all_to_all(finished, 'dev', split_axis=0, concat_axis=0, tiled=True)  10.7 us
    dot_general x1, matrix products, attend_row(): jnp.dot(probs, cache_lat, preferred_element_type=jnp.float32)  6.34 us
    gather x1, local copies, waits for them, and re-layouts, per_device(): flat_back[destination].reshape(tok_count, topk_count, width)  6.04 us
  transfers between devices with their start and end apart: 2, of which 2 were waited for; matrix products, arithmetic and copies ran while one was open for 7% of the time, Pallas kernels for 0%

profile of v1, /device:TPU:1, one launch (start us, length us, event | category | flops | bytes accessed | tf_op | source)
XLA Modules:
  0.0 210.9 jit_solution(12176131654792828475)
XLA Ops:
  7.2 0.8 copy.15
  8.2 0.7 broadcast_multiply_fusion
  9.0 0.6 reduce-window.6
  9.6 0.2 slice_reduce_fusion
  10.0 0.1 fusion.21
  10.1 1.4 scatter_custom_fusion
  11.5 1.0 concatenate.3
  12.5 4.2 %gather_fusion = bf16[512,3584]{1,0:T(8,128)(2,1)} fusion(bf16[33,3584]{1,0:T(8,128)(2,1)S(1)} %concatenate.3, s32[1024]{0:T(1024)S(1)} %pad_clamp_fusion.1), kind=kCustom, calls=%fused_computation | custom fusion | bytes 7342080 | tf_op jit(solution)/shard_map/gather | solution.py:66
  16.6 57.4 %all_to_all.15 = bf16[64,8,3584]{2,1,0:T(8,128)(2,1)S(1)} all-to-all(bf16[64,8,3584]{2,1,0:T(8,128)(2,1)} %bitcast.50), channel_id=1, replica_groups=mesh['role'=2,'dev'=64] {'dev'}, dimensions={0} | all-to-all | bytes 7340032 | tf_op jit(solution)/shard_map/all_to_all | solution.py:67
  74.1 0.6 pad_maximum_fusion
  74.7 11.9 %all_to_all.16 = bf16[2,512,3584]{2,1,0:T(8,128)(2,1)S(1)} all-to-all(bf16[2,512,3584]{2,1,0:T(8,128)(2,1)S(1)} %pad_maximum_fusion), channel_id=1, replica_groups=mesh['role'=2,'dev'=64] {'role'}, dimensions={0} | all-to-all | bytes 14680064 | tf_op jit(solution)/shard_map/all_to_all | solution.py:70
  86.6 2.9 %copy-done.1 = bf16[2,512,3584]{2,1,0:T(8,128)(2,1)} copy-done((bf16[2,512,3584]{2,1,0:T(8,128)(2,1)}, bf16[2,512,3584]{2,1,0:T(8,128)(2,1)S(1)}, u32[]{:S(2)}) %copy-start.1) | copy-done | bytes 7340056
  89.5 3.9 %fusion.4 = f32[1024,512]{1,0:T(8,128)S(1)} fusion(bf16[1024,3584]{1,0:T(8,128)(2,1)S(1)} %bitcast.52, bf16[1,3584,512]{2,1,0:T(8,128)(2,1)S(1)} %copy-done.6), kind=kOutput, calls=%fused_computation.9 | convolution fusion | flops 3758096384 | bytes 13107200 | tf_op jit(solution)/shard_map/dot_general | solution.py:11
  93.5 15.5 %fusion.2 = f32[1024,3584]{1,0:T(8,128)} fusion(bf16[1,3584,512]{2,1,0:T(8,128)(2,1)} %param.16, f32[1024,512]{1,0:T(8,128)S(1)} %fusion.4, bf16[1024,3584]{1,0:T(8,128)(2,1)} %bitcast.53, bf16[1,3584,512]{2,1,0:T(8,128)(2,1)} %param.14), kind=kOutput, calls=%fused_computation.7 | convolution fusion | flops 7519338496 | bytes 31457280 | tf_op jit(solution)/shard_map/dot_general | solution.py:13
  109.0 23.2 %reduce-scatter.2.cloned.1.call-done = f32[512,3584]{1,0:T(8,128)} async-done(((f32[1024,3584]{1,0:T(8,128)}), f32[512,3584]{1,0:T(8,128)}) %reduce-scatter.2.cloned.1.call-update) | async-done | bytes 7340048 | tf_op jit(solution)/shard_map/reduce_scatter | solution.py:72
  132.2 5.3 %convert_bitcast_fusion = bf16[64,8,3584]{2,1,0:T(8,128)(2,1)} fusion(f32[512,3584]{1,0:T(8,128)} %reduce-scatter.2.cloned.1.call-done), kind=kLoop, calls=%fused_computation.13 | loop fusion | flops 1835008 | bytes 11010048 | tf_op jit(solution)/shard_map/reshape | solution.py:78
  137.5 10.7 %all-to-all-start.2 = ((bf16[64,8,3584]{2,1,0:T(8,128)(2,1)}), bf16[64,8,3584]{2,1,0:T(8,128)(2,1)}, u32[]{:S(2)}, u32[]{:S(2)}) async-start(bf16[64,8,3584]{2,1,0:T(8,128)(2,1)} %convert_bitcast_fusion), calls=%async_computation.3 | async-start | bytes 7340032 | tf_op jit(solution)/shard_map/all_to_all | solution.py:79
  148.3 0.1 reshape.93
  148.5 6.0 %fusion.27 = f32[4,64,2048]{2,1,0:T(8,128)S(1)} fusion(bf16[4,64,512]{2,1,0:T(8,128)(2,1)S(1)} %copy-done.2, bf16[4,2048,512]{2,1,0:T(8,128)(2,1)} %param.19), kind=kOutput, calls=%fused_computation.48 | convolution fusion | flops 536870912 | bytes 10747904 | tf_op jit(solution)/shard_map/vmap()/dot_general | solution.py:21
  154.5 2.4 %fusion.26 = (f32[4,64]{1,0:T(4,128)S(1)}, f32[4,64,2048]{2,1,0:T(8,128)}) fusion(pred[4,2048]{1,0:T(4,128)(4,1)S(1)} %iota_compare_fusion.2, f32[4,64,2048]{2,1,0:T(8,128)S(1)} %fusion.27, bf16[4,64,64]{2,1,0:T(8,128)(2,1)S(1)} %reshape.93, bf16[4,64,2048]{2,1,0:T(8,128)(2,1)S(1)} %copy-done), kind=kOutput, calls=%fused_computation.47 | convolution fusion | flops 70256640 | bytes 5284864 | tf_op jit(solution)/shard_map/vmap()/sub | solution.py:32
  156.9 6.3 %convolution_convert_fusion = bf16[4,64,512]{2,1,0:T(8,128)(2,1)} fusion(bf16[4,2048,512]{2,1,0:T(8,128)(2,1)} %param.19, f32[4,64,2048]{2,1,0:T(8,128)} %get-tuple-element.3, f32[4,64]{1,0:T(4,128)S(1)} %get-tuple-element.2), kind=kOutput, calls=%fused_computation.22 | convolution fusion | flops 538050560 | bytes 10748928 | tf_op jit(solution)/shard_map/vmap()/dot_general | solution.py:34
  163.2 32.6 %all-to-all-done.2 = bf16[64,8,3584]{2,1,0:T(8,128)(2,1)} async-done(((bf16[64,8,3584]{2,1,0:T(8,128)(2,1)}), bf16[64,8,3584]{2,1,0:T(8,128)(2,1)}, u32[]{:S(2)}, u32[]{:S(2)}) %all-to-all-start.2) | async-done | bytes 3670048 | tf_op jit(solution)/shard_map/all_to_all | solution.py:79
  195.8 6.0 %gather_fusion.1 = bf16[256,3584]{1,0:T(8,128)(2,1)S(1)} fusion(bf16[512,3584]{1,0:T(8,128)(2,1)} %bitcast.10, s32[1024]{0:T(1024)S(1)} %pad_clamp_fusion), kind=kCustom, calls=%fused_computation.1 | custom fusion | bytes 3671040 | tf_op jit(solution)/shard_map/gather | solution.py:81
  201.9 2.1 %fusion.1 = bf16[32,3584]{1,0:T(8,128)(2,1)} fusion(bf16[256,3584]{1,0:T(8,128)(2,1)S(1)} %gather_fusion.1, f32[32,8]{1,0:T(8,128)S(1)} %copy.18), kind=kLoop, calls=%fused_computation.6 | loop fusion | flops 2637824 | bytes 2065408 | tf_op jit(solution)/shard_map/reduce_sum | solution.py:82
  (29 shorter events, 0.7 us)
Async XLA Ops:
  7.2 147.4 %copy-start = (bf16[4,64,2048]{2,1,0:T(8,128)(2,1)S(1)}, bf16[4,64,2048]{2,1,0:T(8,128)(2,1)}, u32[]{:S(2)}) copy-start(bf16[4,64,2048]{2,1,0:T(8,128)(2,1)} %param.20) | copy-start | bytes 3145732
  7.2 125.0 %reduce-scatter.2.cloned.1.call-start = ((), (), s32[]{:S(2)}) async-start(), calls=%async_computation.4 | async-start | bytes 22020096 | tf_op jit(solution)/shard_map/reduce_scatter | solution.py:72
  74.7 14.9 %copy-start.6 = (bf16[1,3584,512]{2,1,0:T(8,128)(2,1)S(1)}, bf16[1,3584,512]{2,1,0:T(8,128)(2,1)}, u32[]{:S(2)}) copy-start(bf16[1,3584,512]{2,1,0:T(8,128)(2,1)} %param.15) | copy-start | bytes 11010052
  86.6 2.9 %copy-start.1 = (bf16[2,512,3584]{2,1,0:T(8,128)(2,1)}, bf16[2,512,3584]{2,1,0:T(8,128)(2,1)S(1)}, u32[]{:S(2)}) copy-start(bf16[2,512,3584]{2,1,0:T(8,128)(2,1)S(1)} %all_to_all.16) | copy-start | bytes 22020100
  137.5 10.7 %copy-start.4 = (f32[32,8]{0,1:T(8,128)S(1)}, f32[32,8]{0,1:T(8,128)}, u32[]{:S(2)}) copy-start(f32[32,8]{0,1:T(8,128)} %param.13) | copy-start | bytes 3076
  137.5 10.8 %copy-start.3 = (bf16[4,4096]{1,0:T(4,128)(2,1)S(1)}, bf16[4,4096]{1,0:T(4,128)(2,1)}, u32[]{:S(2)}) copy-start(bf16[4,4096]{1,0:T(4,128)(2,1)} %param.18) | copy-start | bytes 98308
  137.5 10.9 %copy-start.5 = (s32[4]{0:T(128)S(1)}, s32[4]{0:T(128)}, u32[]{:S(2)}) copy-start(s32[4]{0:T(128)} %param.21) | copy-start | bytes 52
  137.5 11.0 %copy-start.2 = (bf16[4,64,512]{2,1,0:T(8,128)(2,1)S(1)}, bf16[4,64,512]{2,1,0:T(8,128)(2,1)}, u32[]{:S(2)}) copy-start(bf16[4,64,512]{2,1,0:T(8,128)(2,1)} %param.17) | copy-start | bytes 786436
  137.5 58.3 %all-to-all-start.2 = ((bf16[64,8,3584]{2,1,0:T(8,128)(2,1)}), bf16[64,8,3584]{2,1,0:T(8,128)(2,1)}, u32[]{:S(2)}, u32[]{:S(2)}) async-start(bf16[64,8,3584]{2,1,0:T(8,128)(2,1)} %convert_bitcast_fusion), calls=%async_computation.3 | async-start | bytes 7340032 | tf_op jit(solution)/shard_map/all_to_all | solution.py:79
Sparse Core Ops, SparseCore 0:
  109.1 23.0 reduce-scatter.1
